TPU v7x, 32 devices: a whole 2x2x4 slice. The times are simulated.
32 devices in a mesh: rep: 4 (over z), fsdp: 8 (over y, x, core).
Axes of the slice: x: 2, y: 2, z: 4, core: 2. Of those that a mesh axis runs over, the one named last changes fastest.
Arguments:
- activations: bfloat16 [4, 16384, 4096], P('rep', 'fsdp'), may hold values from -6 to 6
- cotangent: bfloat16 [4, 16384, 1024], P('rep', 'fsdp'), may hold values from -0.046875 to 0.046875
- momentum: float32 [4, 4096, 1024], P('rep', 'fsdp'), may hold values from -6 to 6
Outputs:
- momentum_next: float32 [4, 4096, 1024], P('rep', 'fsdp')
- update: float32 [4096, 1024], P('fsdp')
All inputs are finite; a program needn't handle non-finite values.
Results may differ from a plain program's by a relative error of at most 0.0021.
Values sent between devices are 32-bit elements; how exact they have to be, the bound alone decides.
No kernel may reach another device: no remote copies, remote signals or barrier semaphores. Data moves between devices by JAX's collectives and lax.ppermute only.
A program may use at most 128 MiB of HBM per device.

v0:
```python
import jax
import jax.numpy as jnp
from jax import lax
from jax.sharding import PartitionSpec as P

CH = 64
BAND = 16
momentum_decay = 0.9


def basis_rows(size, keep):
    freq = jnp.arange(keep, dtype=jnp.float32)[:, None]
    point = jnp.arange(size, dtype=jnp.float32)[None, :]
    waves = jnp.cos(jnp.pi * (2.0 * point + 1.0) * freq / (2.0 * size))
    scales = jnp.where(freq == 0.0, jnp.sqrt(1.0 / size), jnp.sqrt(2.0 / size))
    return waves * scales


def bands_of(field, basis):
    rows, width = field.shape
    blocks = field.reshape(rows // CH, CH, width // CH, CH)
    return jnp.einsum("kn,anbm,lm->akbl", basis, blocks, basis, precision=lax.Precision.HIGHEST)


def term_maker(normed, part):
    return lax.dot_general(
        normed, part, (((0,), (0,)), ((), ())), preferred_element_type=jnp.float32
    )


def settle(grad, field, basis):
    accumulated = momentum_decay * field + grad
    bands = bands_of(accumulated, basis)
    count, _, wide, _ = bands.shape
    blocks = jnp.einsum("kn,akbl,lm->anbm", basis, bands, basis, precision=lax.Precision.HIGHEST)
    return (accumulated - blocks.reshape(count * CH, wide * CH), bands)


def body(activations, cotangent, momentum):
    values = activations[0].astype(jnp.float32)
    stat = jnp.mean(values * values, axis=-1, keepdims=True)
    normed = (values * lax.rsqrt(stat + 1e-05)).astype(jnp.bfloat16)
    targets = cotangent[0]
    field = momentum[0]
    basis = basis_rows(CH, BAND)
    grad = lax.psum_scatter(term_maker(normed, targets), "fsdp", scatter_dimension=0, tiled=True)
    cleared, bands = settle(grad, field, basis)
    count, _, wide, _ = bands.shape
    summed = lax.psum(bands, "rep")
    blocks = jnp.einsum("kn,akbl,lm->anbm", basis, summed, basis, precision=lax.Precision.HIGHEST)
    update = blocks.reshape(count * CH, wide * CH)
    groups = lax.axis_size("rep")
    return (cleared[None], update / groups)


def solution(mesh):
    return jax.shard_map(
        body,
        mesh=mesh,
        in_specs=(P("rep", "fsdp", None), P("rep", "fsdp", None), P("rep", "fsdp", None)),
        out_specs=(P("rep", "fsdp", None), P("fsdp", None)),
        check_vma=False,
    )
```

profile of v0, /device:TPU:0, one launch (start us, length us, event | category | flops | bytes accessed | tf_op | source)
XLA Modules:
  0.0 262.0 jit_solution(10249392141727543123)
XLA Ops:
  7.2 0.0 reduce-scatter.2.cloned.1.call-start
  7.2 0.0 copy-start
  7.2 7.6 %fusion = f32[2048]{0:T(1024)S(1)} fusion(bf16[1,2048,4096]{2,1,0:T(8,128)(2,1)} %param.3), kind=kLoop, calls=%fused_computation.2 | loop fusion | flops 25163776 | bytes 16785408 | tf_op jit(solution)/shard_map/reduce_sum | solution.py:41
  14.8 3.1 %copy-done = bf16[1,2048,4096]{2,1,0:T(8,128)(2,1)S(1)} copy-done((bf16[1,2048,4096]{2,1,0:T(8,128)(2,1)S(1)}, bf16[1,2048,4096]{2,1,0:T(8,128)(2,1)}, u32[]{:S(2)}) %copy-start) | copy-done | bytes 16777240
  17.9 23.4 %fusion.3 = f32[4096,1024]{1,0:T(8,128)} fusion(bf16[1,2048,4096]{2,1,0:T(8,128)(2,1)S(1)} %copy-done, f32[2048]{0:T(1024)S(1)} %add_rsqrt_fusion, bf16[1,2048,1024]{2,1,0:T(8,128)(2,1)} %param.4), kind=kOutput, calls=%fused_computation.5 | convolution fusion | flops 17205035008 | bytes 37756928 | tf_op jit(solution)/shard_map/dot_general | solution.py:26
  41.3 0.0 reduce-scatter.2.cloned.1.call-update
  41.3 119.0 %reduce-scatter.2.cloned.1.call-done = f32[512,1024]{1,0:T(8,128)} async-done(((f32[4096,1024]{1,0:T(8,128)}), f32[512,1024]{1,0:T(8,128)}) %reduce-scatter.2.cloned.1.call-update) | async-done | bytes 2097168 | tf_op jit(solution)/shard_map/reduce_scatter | solution.py:46
  160.3 2.7 %bitcast_add_fusion = f32[512,1024]{1,0:T(8,128)S(1)} fusion(f32[512,1024]{1,0:T(8,128)} %reduce-scatter.2.cloned.1.call-done, f32[1,512,1024]{2,1,0:T(8,128)} %param.5), kind=kLoop, calls=%fused_computation.12 | loop fusion | flops 1048576 | bytes 6291456 | tf_op jit(solution)/shard_map/add | solution.py:32
  163.0 2.5 reshape.49
  165.5 5.6 %fusion.7 = f32[8,16,64,16]{2,3,1,0:T(8,128)S(1)} fusion(f32[8,64,16,64]{3,2,1,0:T(8,128)} %reshape.49, f32[16]{0:T(128)S(1)} %compare_select_fusion, f32[64]{0:T(128)S(1)} %add_multiply_fusion), kind=kOutput, calls=%fused_computation.8 | convolution fusion | flops 100666368 | bytes 2621760 | tf_op jit(solution)/shard_map/kn,anbm,lm->akbl/dot_general | solution.py:22
  171.1 1.0 convolution_bitcast_fusion.1
  172.1 0.0 copy-start.1
  172.1 2.8 %fusion.13 = f32[8,16,16,64]{3,2,1,0:T(8,128)} fusion(f32[8,16,16,16]{3,1,2,0:T(8,128)S(1)} %convolution_bitcast_fusion.1, f32[16]{0:T(128)S(1)} %compare_select_fusion, f32[64]{0:T(128)S(1)} %add_multiply_fusion), kind=kOutput, calls=%fused_computation.19 | convolution fusion | flops 25168896 | bytes 655680 | tf_op jit(solution)/shard_map/kn,akbl,lm->anbm/dot_general | solution.py:35
  174.9 0.0 all-reduce.2.cloned.1.call-start
  174.9 9.3 %convolution_bitcast_fusion = f32[8,64,16,64]{3,1,2,0:T(8,128)} fusion(f32[8,16,16,64]{3,2,1,0:T(8,128)} %fusion.13, f32[16]{0:T(128)S(1)} %compare_select_fusion, f32[64]{0:T(128)S(1)} %add_multiply_fusion), kind=kOutput, calls=%fused_computation.11 | convolution fusion | flops 100666368 | bytes 2621760 | tf_op jit(solution)/shard_map/kn,akbl,lm->anbm/dot_general | solution.py:35
  184.2 0.0 copy-done.1
  184.2 0.0 all-reduce.2.cloned.1.call-update
  184.2 6.5 %copy.6 = f32[8,64,16,64]{3,2,1,0:T(8,128)} copy(f32[8,64,16,64]{3,1,2,0:T(8,128)} %convolution_bitcast_fusion) | data formatting | bytes 4194304 | tf_op jit(solution)/shard_map/kn,akbl,lm->anbm/transpose | solution.py:35
  190.8 4.8 %reshape.50 = f32[512,1024]{1,0:T(8,128)} reshape(f32[8,64,16,64]{3,2,1,0:T(8,128)} %copy.6) | data formatting | bytes 4194304 | tf_op jit(solution)/shard_map/reshape | solution.py:36
  195.6 3.3 %subtract_bitcast_fusion = f32[1,512,1024]{2,1,0:T(8,128)} fusion(f32[512,1024]{1,0:T(8,128)S(1)} %bitcast_add_fusion, f32[512,1024]{1,0:T(8,128)} %reshape.50), kind=kLoop, calls=%fused_computation.13 | loop fusion | flops 524288 | bytes 6291456 | tf_op jit(solution)/shard_map/broadcast_in_dim | solution.py:53
  198.9 37.4 %all-reduce.2.cloned.1.call-done = f32[8,16,16,16]{3,1,2,0:T(8,128)} async-done(((f32[8,16,16,16]{3,1,2,0:T(8,128)}), f32[8,16,16,16]{3,1,2,0:T(8,128)}) %all-reduce.2.cloned.1.call-update) | async-done | bytes 131088 | tf_op jit(solution)/shard_map/psum | solution.py:49
  236.3 3.0 %fusion.10 = f32[8,16,16,64]{3,2,1,0:T(8,128)S(1)} fusion(f32[8,16,16,16]{3,1,2,0:T(8,128)} %all-reduce.2.cloned.1.call-done, f32[16]{0:T(128)S(1)} %compare_select_fusion, f32[64]{0:T(128)S(1)} %add_multiply_fusion), kind=kOutput, calls=%fused_computation.16 | convolution fusion | flops 25168896 | bytes 655680 | tf_op jit(solution)/shard_map/kn,akbl,lm->anbm/dot_general | solution.py:50
  239.3 6.7 %multiply_bitcast_fusion = f32[8,64,16,64]{3,1,2,0:T(8,128)S(1)} fusion(f32[8,16,16,64]{3,2,1,0:T(8,128)S(1)} %fusion.10, f32[16]{0:T(128)S(1)} %compare_select_fusion, f32[64]{0:T(128)S(1)} %add_multiply_fusion), kind=kOutput, calls=%fused_computation.10 | convolution fusion | flops 101190656 | bytes 2621760 | tf_op jit(solution)/shard_map/kn,akbl,lm->anbm/dot_general | solution.py:50
  246.1 4.3 %copy.7 = f32[8,64,16,64]{3,2,1,0:T(8,128)} copy(f32[8,64,16,64]{3,1,2,0:T(8,128)S(1)} %multiply_bitcast_fusion) | data formatting | bytes 4194304 | tf_op jit(solution)/shard_map/div | solution.py:53
  250.4 4.8 %div.39 = f32[512,1024]{1,0:T(8,128)} reshape(f32[8,64,16,64]{3,2,1,0:T(8,128)} %copy.7) | data formatting | bytes 4194304 | tf_op jit(solution)/shard_map/div | solution.py:53
  (3 shorter events, 0.0 us)
Async XLA Ops:
  7.2 153.2 %reduce-scatter.2.cloned.1.call-start = ((), (), s32[]{:S(2)}) async-start(), calls=%async_computation.1 | async-start | bytes 18874368 | tf_op jit(solution)/shard_map/reduce_scatter | solution.py:46
  7.2 10.7 %copy-start = (bf16[1,2048,4096]{2,1,0:T(8,128)(2,1)S(1)}, bf16[1,2048,4096]{2,1,0:T(8,128)(2,1)}, u32[]{:S(2)}) copy-start(bf16[1,2048,4096]{2,1,0:T(8,128)(2,1)} %param.3) | copy-start | bytes 50331652
  172.1 12.1 %copy-start.1 = (f32[8,16,16,16]{3,1,2,0:T(8,128)}, f32[8,16,16,16]{3,1,2,0:T(8,128)S(1)}, u32[]{:S(2)}) copy-start(f32[8,16,16,16]{3,1,2,0:T(8,128)S(1)} %convolution_bitcast_fusion.1) | copy-start | bytes 393220
  174.9 61.4 %all-reduce.2.cloned.1.call-start = ((), (), s32[]{:S(2)}) async-start(), calls=%async_computation.2 | async-start | bytes 2097152 | tf_op jit(solution)/shard_map/psum | solution.py:49
Sparse Core Ops, SparseCore 0:
  41.4 118.8 reduce-scatter.1
  184.4 51.8 all-reduce.1
where the time goes:
time: 262 us
  waiting for transfers between devices  156 us (60%)
  matrix products  51.8 us (20%)
  local copies, waits for them, and re-layouts  26.1 us (10%)
  between operations  14.1 us (5%)
  other arithmetic  13.6 us (5%)
    reduce_scatter x1, waiting for transfers between devices, body(): lax.psum_scatter(term_maker(normed, targets), 'fsdp', scatter_dimension=0...  119 us
    psum x1, waiting for transfers between devices, body(): summed = lax.psum(bands, 'rep')  37.4 us
    dot_general x1, matrix products, term_maker(): lax.dot_general(normed, part, (((0,), (0,)), ((), ())), preferred_element...  23.4 us
    dot_general x2, matrix products, settle(): jnp.einsum('kn,akbl,lm->anbm', basis, bands, basis, precision=lax.Precisi...  12.1 us
    dot_general x2, matrix products, body(): jnp.einsum('kn,akbl,lm->anbm', basis, summed, basis, precision=lax.Precis...  9.76 us
    div x2, local copies, waits for them, and re-layouts, body(): return (cleared[None], update / groups)  9.14 us
    reduce_sum x1, other arithmetic, body(): stat = jnp.mean(values * values, axis=-1, keepdims=True)  7.6 us
    dot_general x2, matrix products, bands_of(): jnp.einsum('kn,anbm,lm->akbl', basis, blocks, basis, precision=lax.Precis...  6.6 us
  transfers between devices with their start and end apart: 2, of which 2 were waited for; matrix products, arithmetic and copies ran while one was open for 6% of the time, Pallas kernels for 0%

commit v1 on v0

--- a/solution.py
+++ b/solution.py
@@ -46,7 +46,11 @@
     grad = lax.psum_scatter(term_maker(normed, targets), "fsdp", scatter_dimension=0, tiled=True)
     cleared, bands = settle(grad, field, basis)
     count, _, wide, _ = bands.shape
-    summed = lax.psum(bands, "rep")
+    n_dev = lax.axis_size("rep")
+    summed, reach = (bands, 1)
+    while reach < n_dev:
+        summed = summed + lax.ppermute(summed, "rep", [(i, i ^ reach) for i in range(n_dev)])
+        reach = 2 * reach
     blocks = jnp.einsum("kn,akbl,lm->anbm", basis, summed, basis, precision=lax.Precision.HIGHEST)
     update = blocks.reshape(count * CH, wide * CH)
     groups = lax.axis_size("rep")

time: 262 us -> 273 us (1.042)
  waiting for transfers between devices: 156 us -> 170 us
  matrix products: 51.8 us -> 47.3 us
  starting transfers between devices: 0.04 us -> 4.04 us
    ppermute x0 -> x2, waiting for transfers between devices: none -> 50.7 us  [body(): lax.ppermute(summed, 'rep', [(i, i ^ reach) for i in range(n_dev)])]
    psum x1 -> x0, waiting for transfers between devices: 37.4 us -> none  [body(): summed = lax.psum(bands, 'rep')]
    ppermute x0 -> x2, starting transfers between devices: none -> 4 us  [body(): lax.ppermute(summed, 'rep', [(i, i ^ reach) for i in range(n_dev)])]
    dot_general x2, matrix products: 12.1 us -> 8.54 us  [settle(): jnp.einsum('kn,akbl,lm->anbm', basis, bands, basis, precision=lax.Precisi...]
  transfers between devices with their start and end apart: 2 -> 3, of which waited for: 2 -> 3; matrix products, arithmetic and copies ran while one was open for 6% -> 6% of each run, Pallas kernels for 0% -> 0%
where the time goes in v1:
time: 273 us; the launch traced here: 272 us
  waiting for transfers between devices  170 us (62%)
  matrix products  47.3 us (17%)
  local copies, waits for them, and re-layouts  23.9 us (9%)
  between operations  14.1 us (5%)
  other arithmetic  13.4 us (5%)
  starting transfers between devices  4.04 us (1%)
    reduce_scatter x1, waiting for transfers between devices, body(): lax.psum_scatter(term_maker(normed, targets), 'fsdp', scatter_dimension=0...  119 us
    ppermute x2, waiting for transfers between devices, body(): lax.ppermute(summed, 'rep', [(i, i ^ reach) for i in range(n_dev)])  50.7 us
    dot_general x1, matrix products, term_maker(): lax.dot_general(normed, part, (((0,), (0,)), ((), ())), preferred_element...  23.4 us
    div x2, local copies, waits for them, and re-layouts, body(): return (cleared[None], update / groups)  9.15 us
    dot_general x2, matrix products, body(): jnp.einsum('kn,akbl,lm->anbm', basis, summed, basis, precision=lax.Precis...  8.6 us
    dot_general x2, matrix products, settle(): jnp.einsum('kn,akbl,lm->anbm', basis, bands, basis, precision=lax.Precisi...  8.54 us
    reduce_sum x1, other arithmetic, body(): stat = jnp.mean(values * values, axis=-1, keepdims=True)  7.6 us
    dot_general x2, matrix products, bands_of(): jnp.einsum('kn,anbm,lm->akbl', basis, blocks, basis, precision=lax.Precis...  6.78 us
  transfers between devices with their start and end apart: 3, of which 3 were waited for; matrix products, arithmetic and copies ran while one was open for 6% of the time, Pallas kernels for 0%

profile of v1, /device:TPU:0, one launch (start us, length us, event | category | flops | bytes accessed | tf_op | source)
XLA Modules:
  0.0 272.4 jit_solution(1504084400739425403)
XLA Ops:
  7.2 0.0 reduce-scatter.2.cloned.1.call-start
  7.2 0.0 copy-start
  7.2 7.6 %fusion = f32[2048]{0:T(1024)S(1)} fusion(bf16[1,2048,4096]{2,1,0:T(8,128)(2,1)} %param.3), kind=kLoop, calls=%fused_computation.2 | loop fusion | flops 25163776 | bytes 16785408 | tf_op jit(solution)/shard_map/reduce_sum | solution.py:41
  14.8 3.1 %copy-done = bf16[1,2048,4096]{2,1,0:T(8,128)(2,1)S(1)} copy-done((bf16[1,2048,4096]{2,1,0:T(8,128)(2,1)S(1)}, bf16[1,2048,4096]{2,1,0:T(8,128)(2,1)}, u32[]{:S(2)}) %copy-start) | copy-done | bytes 16777240
  17.9 23.4 %fusion.3 = f32[4096,1024]{1,0:T(8,128)} fusion(bf16[1,2048,4096]{2,1,0:T(8,128)(2,1)S(1)} %copy-done, f32[2048]{0:T(1024)S(1)} %add_rsqrt_fusion, bf16[1,2048,1024]{2,1,0:T(8,128)(2,1)} %param.4), kind=kOutput, calls=%fused_computation.5 | convolution fusion | flops 17205035008 | bytes 37756928 | tf_op jit(solution)/shard_map/dot_general | solution.py:26
  41.3 0.0 reduce-scatter.2.cloned.1.call-update
  41.3 119.0 %reduce-scatter.2.cloned.1.call-done = f32[512,1024]{1,0:T(8,128)} async-done(((f32[4096,1024]{1,0:T(8,128)}), f32[512,1024]{1,0:T(8,128)}) %reduce-scatter.2.cloned.1.call-update) | async-done | bytes 2097168 | tf_op jit(solution)/shard_map/reduce_scatter | solution.py:46
  160.3 2.7 bitcast_add_fusion
  163.0 2.5 reshape.49
  165.5 5.8 %fusion.7 = f32[8,16,64,16]{2,3,1,0:T(8,128)S(1)} fusion(f32[8,64,16,64]{3,2,1,0:T(8,128)} %reshape.49, f32[16]{0:T(128)S(1)} %compare_select_fusion, f32[64]{0:T(128)S(1)} %add_multiply_fusion), kind=kOutput, calls=%fused_computation.8 | convolution fusion | flops 100666368 | bytes 2621760 | tf_op jit(solution)/shard_map/kn,anbm,lm->akbl/dot_general | solution.py:22
  171.3 1.0 convolution_bitcast_fusion.1
  172.3 1.8 fusion.14
  174.1 1.6 collective-permute-start
  175.7 6.7 %convolution_bitcast_fusion = f32[8,64,16,64]{3,1,2,0:T(8,128)S(1)} fusion(f32[8,16,16,64]{3,2,1,0:T(8,128)S(1)} %fusion.14, f32[16]{0:T(128)S(1)} %compare_select_fusion, f32[64]{0:T(128)S(1)} %add_multiply_fusion), kind=kOutput, calls=%fused_computation.11 | convolution fusion | flops 100666368 | bytes 2621760 | tf_op jit(solution)/shard_map/kn,akbl,lm->anbm/dot_general | solution.py:35
  182.4 4.3 %copy.6 = f32[8,64,16,64]{3,2,1,0:T(8,128)} copy(f32[8,64,16,64]{3,1,2,0:T(8,128)S(1)} %convolution_bitcast_fusion) | data formatting | bytes 4194304 | tf_op jit(solution)/shard_map/kn,akbl,lm->anbm/transpose | solution.py:35
  186.7 4.8 %reshape.50 = f32[512,1024]{1,0:T(8,128)} reshape(f32[8,64,16,64]{3,2,1,0:T(8,128)} %copy.6) | data formatting | bytes 4194304 | tf_op jit(solution)/shard_map/reshape | solution.py:36
  191.6 0.0 copy-start.1
  191.6 7.5 %collective-permute-done = f32[8,16,16,16]{3,1,2,0:T(8,128)} collective-permute-done((f32[8,16,16,16]{3,1,2,0:T(8,128)S(1)}, f32[8,16,16,16]{3,1,2,0:T(8,128)}, u32[]{:S(2)}, u32[]{:S(2)}) %collective-permute-start) | collective-permute-done | bytes 131104 | tf_op jit(solution)/shard_map/ppermute | solution.py:52
  199.1 1.4 add.48
  200.4 2.5 collective-permute-start.1
  202.9 0.0 copy-done.1
  202.9 1.7 subtract_bitcast_fusion
  204.6 43.2 %collective-permute-done.1 = f32[8,16,16,16]{3,1,2,0:T(8,128)S(1)} collective-permute-done((f32[8,16,16,16]{3,1,2,0:T(8,128)S(1)}, f32[8,16,16,16]{3,1,2,0:T(8,128)S(1)}, u32[]{:S(2)}, u32[]{:S(2)}) %collective-permute-start.1) | collective-permute-done | bytes 131104 | tf_op jit(solution)/shard_map/ppermute | solution.py:52
  247.7 1.8 fusion.9
  249.6 6.8 %multiply_bitcast_fusion = f32[8,64,16,64]{3,1,2,0:T(8,128)S(1)} fusion(f32[8,16,16,64]{3,2,1,0:T(8,128)S(1)} %fusion.9, f32[16]{0:T(128)S(1)} %compare_select_fusion, f32[64]{0:T(128)S(1)} %add_multiply_fusion), kind=kOutput, calls=%fused_computation.10 | convolution fusion | flops 101190656 | bytes 2621760 | tf_op jit(solution)/shard_map/kn,akbl,lm->anbm/dot_general | solution.py:54
  256.4 4.3 %copy.7 = f32[8,64,16,64]{3,2,1,0:T(8,128)} copy(f32[8,64,16,64]{3,1,2,0:T(8,128)S(1)} %multiply_bitcast_fusion) | data formatting | bytes 4194304 | tf_op jit(solution)/shard_map/div | solution.py:57
  260.7 4.8 %div.39 = f32[512,1024]{1,0:T(8,128)} reshape(f32[8,64,16,64]{3,2,1,0:T(8,128)} %copy.7) | data formatting | bytes 4194304 | tf_op jit(solution)/shard_map/div | solution.py:57
  (3 shorter events, 0.0 us)
Async XLA Ops:
  7.2 153.2 %reduce-scatter.2.cloned.1.call-start = ((), (), s32[]{:S(2)}) async-start(), calls=%async_computation.1 | async-start | bytes 18874368 | tf_op jit(solution)/shard_map/reduce_scatter | solution.py:46
  7.2 10.7 %copy-start = (bf16[1,2048,4096]{2,1,0:T(8,128)(2,1)S(1)}, bf16[1,2048,4096]{2,1,0:T(8,128)(2,1)}, u32[]{:S(2)}) copy-start(bf16[1,2048,4096]{2,1,0:T(8,128)(2,1)} %param.3) | copy-start | bytes 50331652
  174.1 24.9 %collective-permute-start = (f32[8,16,16,16]{3,1,2,0:T(8,128)S(1)}, f32[8,16,16,16]{3,1,2,0:T(8,128)}, u32[]{:S(2)}, u32[]{:S(2)}) collective-permute-start(f32[8,16,16,16]{3,1,2,0:T(8,128)S(1)} %convolution_bitcast_fusion.1), channel_id=1, source_target_pairs={{0,8},{8,0},{16,24},{24,16},{1,9},{9,1},{17,25},{25,17},{2,10},{10... | collective-permute-start | bytes 393224 | tf_op jit(solution)/shard_map/ppermute | solution.py:52
  191.6 11.3 %copy-start.1 = (f32[512,1024]{1,0:T(8,128)S(1)}, f32[512,1024]{1,0:T(8,128)}, u32[]{:S(2)}) copy-start(f32[512,1024]{1,0:T(8,128)} %reshape.50) | copy-start | bytes 6291460
  200.4 47.3 %collective-permute-start.1 = (f32[8,16,16,16]{3,1,2,0:T(8,128)S(1)}, f32[8,16,16,16]{3,1,2,0:T(8,128)S(1)}, u32[]{:S(2)}, u32[]{:S(2)}) collective-permute-start(f32[8,16,16,16]{3,1,2,0:T(8,128)S(1)} %add.48), channel_id=1, source_target_pairs={{0,16},{8,24},{16,0},{24,8},{1,17},{9,25},{17,1},{25,9},{2,18},{10... | collective-permute-start | bytes 393224 | tf_op jit(solution)/shard_map/ppermute | solution.py:52
Sparse Core Ops, SparseCore 0:
  41.4 118.8 reduce-scatter.1
